TPU v7x, 128 devices: a whole 4x4x4 slice. The times are simulated.
128 devices in a mesh: shard: 16 (over z, x), tensor: 8 (over y, core).
Axes of the slice: x: 4, y: 4, z: 4, core: 2. Of those that a mesh axis runs over, the one named last changes fastest.
Arguments:
- gradient: bfloat16 [768, 3072], P('shard', 'tensor'), may hold values from -12 to 12
- moment_one: float32 [768, 3072], P('shard', 'tensor'), may hold values from -6 to 6
- moment_two: float32 [768, 3072], P('shard', 'tensor'), may hold values from 0.5 to 8
- stat_left: float32 [768, 768], P('shard'), may hold values from -1 to 3, as said below
- stat_right: float32 [3072, 3072], P('shard', 'tensor'), may hold values from -1 to 3, as said below
- basis_left: float32 [768, 768], P('shard'), may hold values from -3 to 25, as said below
- basis_right: float32 [3072, 3072], P('shard', 'tensor'), may hold values from -3 to 47, as said below
Outputs:
- update: bfloat16 [768, 3072], P('shard', 'tensor')
- new_moment_one: float32 [768, 3072], P('shard', 'tensor')
- new_moment_two: float32 [768, 3072], P('shard', 'tensor')
- new_stat_left: float32 [768, 768], P('shard')
- new_stat_right: float32 [3072, 3072], P('shard', 'tensor')
- new_basis_left: float32 [768, 768], P('shard')
- new_basis_right: float32 [3072, 3072], P('shard', 'tensor')
Inputs may be any that keep to these rules, and one draw needn't show every extreme that they name: `stat_left`: symmetric and positive definite. `stat_right`: symmetric and positive definite. `basis_left`: full rank. `basis_right`: full rank.
All inputs are finite; a program needn't handle non-finite values.
Results may differ from a plain program's by a relative error of at most 0.011.
Values may be sent and summed in bfloat16 or wider, within the bound.
A program may use at most 64 MiB of HBM per device.

v0:
```python
import math
import jax
import jax.numpy as jnp
from jax import lax
from jax.sharding import PartitionSpec as P

D = 768
FF = 3072
NS_STEPS = 2
beta_one = 0.95
beta_two = 0.95
beta_stat = 0.95
correction = 1.0 - 0.95**10
adam_eps = 1e-08
highest = lax.Precision.HIGHEST


def blend_stat(previous, product, divisor):
    return beta_stat * previous + (1.0 - beta_stat) * (product / divisor)


def adam_moments(rotated, moment_one, moment_two):
    first_moment = beta_one * moment_one + (1.0 - beta_one) * rotated
    second_moment = beta_two * moment_two + (1.0 - beta_two) * (rotated * rotated)
    direction = (
        first_moment / correction / (jnp.sqrt(second_moment / correction) + adam_eps)
    ).astype(jnp.bfloat16)
    return (first_moment, second_moment, direction)


def local(gradient, moment_one, moment_two, stat_left, stat_right, basis_left, basis_right):
    rows_left = gradient.shape[0]
    rows_right = stat_right.shape[0]
    cols_right = stat_right.shape[1]
    shard_pos = lax.axis_index("shard")
    tensor_pos = lax.axis_index("tensor")
    row_start = shard_pos * rows_left
    grad_cols = lax.all_gather(gradient, "shard", axis=0, tiled=True)
    left_terms = jnp.dot(gradient, grad_cols.T, preferred_element_type=jnp.float32)
    gram_rows = lax.psum(left_terms.astype(jnp.bfloat16), "tensor").astype(jnp.float32)
    new_stat_left = blend_stat(stat_left, gram_rows, FF)
    grad_rows = lax.all_gather(gradient, "tensor", axis=1, tiled=True)
    gram_block = lax.psum_scatter(
        jnp.dot(grad_rows.T, gradient, preferred_element_type=jnp.float32).astype(jnp.bfloat16),
        "shard",
        scatter_dimension=0,
        tiled=True,
    ).astype(jnp.float32)
    new_stat_right = blend_stat(stat_right, gram_block, D)
    basis_all = lax.all_gather(basis_left, "shard", axis=0, tiled=True)
    left_q_all = basis_all / math.sqrt(D)
    left_qb_all = left_q_all.astype(jnp.bfloat16)
    left_qb_own = lax.dynamic_slice_in_dim(left_qb_all, row_start, rows_left, 0)
    left_cols_own = lax.dynamic_slice_in_dim(left_qb_all, row_start, rows_left, 1)
    half_rotated = jnp.dot(left_cols_own.T, grad_cols, preferred_element_type=jnp.float32).astype(
        jnp.bfloat16
    )
    right_q = basis_right / math.sqrt(FF)
    right_qb = right_q.astype(jnp.bfloat16)
    right_cols_b = lax.all_gather(right_qb, "shard", axis=0, tiled=True)
    half_full = lax.all_gather(half_rotated, "tensor", axis=1, tiled=True)
    rotated = jnp.dot(half_full, right_cols_b, preferred_element_type=jnp.float32)
    new_moment_one, new_moment_two, direction = adam_moments(rotated, moment_one, moment_two)
    back_half = jnp.dot(
        left_qb_own,
        lax.all_gather(direction, "shard", axis=0, tiled=True),
        preferred_element_type=jnp.float32,
    ).astype(jnp.bfloat16)
    back_terms = jnp.dot(back_half, right_cols_b.T, preferred_element_type=jnp.float32)
    update = lax.psum_scatter(back_terms, "tensor", scatter_dimension=1, tiled=True).astype(
        jnp.bfloat16
    )
    stat_rows = lax.all_gather(new_stat_right, "tensor", axis=1, tiled=True)
    power_right = jnp.dot(
        stat_rows,
        lax.all_gather(right_q, "shard", axis=0, tiled=True),
        precision=highest,
        preferred_element_type=jnp.float32,
    )
    power_left = jnp.dot(
        new_stat_left, left_q_all, precision=highest, preferred_element_type=jnp.float32
    )
    local_left = jnp.sum(power_left * power_left)
    local_right = jnp.sum(power_right * power_right)
    total_left = lax.psum(local_left, "shard")
    total_right = lax.psum(local_right, ("shard", "tensor"))
    iterate_left = power_left * (math.sqrt(D) / (4.0 * jnp.sqrt(total_left)))
    for iteration in range(NS_STEPS):
        partial_gram = jnp.dot(
            iterate_left.T, iterate_left, precision=highest, preferred_element_type=jnp.float32
        )
        gram_left = lax.psum(partial_gram.astype(jnp.bfloat16), "shard").astype(jnp.float32)
        iterate_left = 1.5 * iterate_left - 0.5 * jnp.dot(
            iterate_left, gram_left, precision=highest, preferred_element_type=jnp.float32
        )
    iterate_right = power_right * (math.sqrt(FF) / (4.0 * jnp.sqrt(total_right)))
    row_ids = shard_pos * rows_right + lax.broadcasted_iota(jnp.int32, (rows_right, cols_right), 0)
    col_ids = tensor_pos * cols_right + lax.broadcasted_iota(jnp.int32, (rows_right, cols_right), 1)
    identity_tile = (row_ids == col_ids).astype(jnp.float32)
    for iteration in range(NS_STEPS):
        rounded_iterate = iterate_right.astype(jnp.bfloat16)
        iterate_rows = lax.all_gather(rounded_iterate, "tensor", axis=1, tiled=True)
        gram_right = lax.psum_scatter(
            jnp.dot(iterate_rows.T, rounded_iterate, preferred_element_type=jnp.float32).astype(
                jnp.bfloat16
            ),
            "shard",
            scatter_dimension=0,
            tiled=True,
        ).astype(jnp.float32)
        mixing = (1.5 * identity_tile - 0.5 * gram_right).astype(jnp.bfloat16)
        iterate_right = jnp.dot(
            iterate_rows,
            lax.all_gather(mixing, "shard", axis=0, tiled=True),
            preferred_element_type=jnp.float32,
        )
    return (
        update,
        new_moment_one,
        new_moment_two,
        new_stat_left,
        new_stat_right,
        iterate_left * math.sqrt(D),
        iterate_right * math.sqrt(FF),
    )


def solution(mesh):
    placed = (
        P("shard", "tensor"),
        P("shard", "tensor"),
        P("shard", "tensor"),
        P("shard", None),
        P("shard", "tensor"),
        P("shard", None),
        P("shard", "tensor"),
    )
    return jax.shard_map(
        local,
        mesh=mesh,
        in_specs=placed,
        out_specs=(
            P("shard", "tensor"),
            P("shard", "tensor"),
            P("shard", "tensor"),
            P("shard", None),
            P("shard", "tensor"),
            P("shard", None),
            P("shard", "tensor"),
        ),
        check_vma=False,
    )
```

profile of v0, /device:TPU:0, one launch (start us, length us, event | category | flops | bytes accessed | tf_op | source)
XLA Modules:
  0.0 935.4 jit_solution(6653130991982937467)
XLA Ops:
  7.2 13.8 %all_gather.41 = bf16[48,3072]{1,0:T(8,128)(2,1)S(1)} all-gather(bf16[48,384]{1,0:T(8,128)(2,1)} %param.7), channel_id=1, replica_groups=mesh['shard'=16,'tensor'=8] {'tensor'}, dimensions={1}, use_global_device_ids=true | all-gather | bytes 331776 | tf_op jit(solution)/shard_map/all_gather | solution.py:42
  21.0 3.1 convolution_convert_fusion.2
  24.1 77.6 %reduce-scatter.7.cloned.1.call-done = bf16[192,384]{1,0:T(8,128)(2,1)} async-done(((bf16[3072,384]{1,0:T(8,128)(2,1)}), bf16[192,384]{1,0:T(8,128)(2,1)}) %reduce-scatter.7.cloned.1.call-update) | async-done | bytes 147472 | tf_op jit(solution)/shard_map/reduce_scatter | solution.py:43
  104.4 24.5 %all-gather.13.cloned.1.call-done = f32[192,3072]{1,0:T(8,128)} async-done(((f32[192,384]{1,0:T(8,128)}), f32[192,3072]{1,0:T(8,128)}) %all-gather.13.cloned.1.call-update) | async-done | bytes 2359312 | tf_op jit(solution)/shard_map/all_gather | solution.py:73
  128.9 57.2 %all-gather.15.cloned.1.call-done = f32[3072,384]{1,0:T(8,128)} async-done(((f32[192,384]{1,0:T(8,128)}), f32[3072,384]{1,0:T(8,128)}) %all-gather.15.cloned.1.call-update) | async-done | bytes 4718608 | tf_op jit(solution)/shard_map/all_gather | solution.py:76
  186.1 7.8 multiply_reduce_fusion
  193.9 64.5 %psum.39 = f32[]{:T(128)} all-reduce(f32[]{:T(128)} %get-tuple-element.14), channel_id=1, replica_groups=mesh['shard'=16,'tensor'=8] {'shard','tensor'}, use_global_device_ids=true, to_apply=%region_8.0 | all-reduce | flops 1 | bytes 8 | tf_op jit(solution)/shard_map/psum | solution.py:86
  259.9 21.0 %all-gather.17.cloned.1.call-done = bf16[192,3072]{1,0:T(8,128)(2,1)} async-done(((bf16[192,384]{1,0:T(8,128)(2,1)}), bf16[192,3072]{1,0:T(8,128)(2,1)}) %all-gather.17.cloned.1.call-update) | async-done | bytes 1179664 | tf_op jit(solution)/shard_map/all_gather | solution.py:102
  280.9 3.7 convolution_convert_fusion.1
  284.7 75.9 %reduce-scatter.9.cloned.1.call-done = bf16[192,384]{1,0:T(8,128)(2,1)} async-done(((bf16[3072,384]{1,0:T(8,128)(2,1)}), bf16[192,384]{1,0:T(8,128)(2,1)}) %reduce-scatter.9.cloned.1.call-update) | async-done | bytes 147472 | tf_op jit(solution)/shard_map/reduce_scatter | solution.py:103
  362.3 23.6 %all_gather.37 = bf16[768,384]{1,0:T(8,128)(2,1)S(1)} all-gather(bf16[48,384]{1,0:T(8,128)(2,1)S(1)} %copy-done.7), channel_id=1, replica_groups=mesh['shard'=16,'tensor'=8] {'shard'}, dimensions={0}, use_global_device_ids=true | all-gather | bytes 626688 | tf_op jit(solution)/shard_map/all_gather | solution.py:38
  387.7 21.1 %all-gather.19.cloned.1.call-done = bf16[3072,384]{1,0:T(8,128)(2,1)} async-done(((bf16[192,384]{1,0:T(8,128)(2,1)}), bf16[3072,384]{1,0:T(8,128)(2,1)}) %all-gather.19.cloned.1.call-update) | async-done | bytes 2359312 | tf_op jit(solution)/shard_map/all_gather | solution.py:114
  408.7 3.1 convolution_convert_fusion.5
  412.5 53.3 %all-reduce.4.cloned.1.call-done = bf16[48,768]{1,0:T(8,128)(2,1)} async-done(((bf16[48,768]{1,0:T(8,128)(2,1)}), bf16[48,768]{1,0:T(8,128)(2,1)}) %all-reduce.4.cloned.1.call-update) | async-done | bytes 73744 | tf_op jit(solution)/shard_map/psum | solution.py:40
  466.8 47.2 %all-gather.9.cloned.1.call-done = f32[768,768]{1,0:T(8,128)} async-done(((f32[48,768]{1,0:T(8,128)}), f32[768,768]{1,0:T(8,128)}) %all-gather.9.cloned.1.call-update) | async-done | bytes 2359312 | tf_op jit(solution)/shard_map/all_gather | solution.py:50
  513.9 3.8 multiply_reduce_fusion.1
  517.7 39.0 %psum.36 = f32[]{:T(128)} all-reduce(f32[]{:T(128)} %get-tuple-element.12), channel_id=1, replica_groups=mesh['shard'=16,'tensor'=8] {'shard'}, use_global_device_ids=true, to_apply=%region_4.0 | all-reduce | flops 1 | bytes 8 | tf_op jit(solution)/shard_map/psum | solution.py:85
  557.5 3.1 convolution_convert_fusion.4
  560.7 3.9 convolution_convert_fusion
  565.9 13.2 %all_gather.38 = bf16[48,3072]{1,0:T(8,128)(2,1)S(1)} all-gather(bf16[48,384]{1,0:T(8,128)(2,1)S(1)} %convolution_convert_fusion.8), channel_id=1, replica_groups=mesh['shard'=16,'tensor'=8] {'tensor'}, dimensions={1}, use_global_device_ids=true | all-gather | bytes 331776 | tf_op jit(solution)/shard_map/all_gather | solution.py:61
  579.2 8.1 all-gather.11.cloned.1.call-done
  587.3 3.0 divide_convert_fusion
  590.2 24.4 %all_gather.40 = bf16[768,384]{1,0:T(8,128)(2,1)S(1)} all-gather(bf16[48,384]{1,0:T(8,128)(2,1)S(1)} %get-tuple-element.7), channel_id=1, replica_groups=mesh['shard'=16,'tensor'=8] {'shard'}, dimensions={0}, use_global_device_ids=true | all-gather | bytes 626688 | tf_op jit(solution)/shard_map/all_gather | solution.py:66
  614.6 2.7 fusion.6
  617.4 60.1 %all-reduce.6.cloned.1.call-done = bf16[768,768]{1,0:T(8,128)(2,1)} async-done(((bf16[768,768]{1,0:T(8,128)(2,1)}), bf16[768,768]{1,0:T(8,128)(2,1)}) %all-reduce.6.cloned.1.call-update) | async-done | bytes 1179664 | tf_op jit(solution)/shard_map/psum | solution.py:92
  679.4 3.1 convolution_convert_fusion.3
  682.6 73.2 %reduce-scatter.11.cloned.1.call-done = bf16[192,384]{1,0:T(8,128)(2,1)} async-done(((bf16[3072,384]{1,0:T(8,128)(2,1)}), bf16[192,384]{1,0:T(8,128)(2,1)}) %reduce-scatter.11.cloned.1.call-update) | async-done | bytes 147472 | tf_op jit(solution)/shard_map/reduce_scatter | solution.py:103
  757.5 31.4 %reduce-scatter.5.cloned.1.call-done = f32[48,384]{1,0:T(8,128)} async-done(((f32[48,3072]{1,0:T(8,128)}), f32[48,384]{1,0:T(8,128)}) %reduce-scatter.5.cloned.1.call-update) | async-done | bytes 73744 | tf_op jit(solution)/shard_map/reduce_scatter | solution.py:70
  790.5 87.6 %all-reduce.8.cloned.1.call-done = bf16[768,768]{1,0:T(8,128)(2,1)} async-done(((bf16[768,768]{1,0:T(8,128)(2,1)}), bf16[768,768]{1,0:T(8,128)(2,1)}) %all-reduce.8.cloned.1.call-update) | async-done | bytes 1179664 | tf_op jit(solution)/shard_map/psum | solution.py:92
  878.1 2.6 fusion.4
  880.7 45.0 %all-gather.23.cloned.1.call-done = bf16[3072,384]{1,0:T(8,128)(2,1)} async-done(((bf16[192,384]{1,0:T(8,128)(2,1)}), bf16[3072,384]{1,0:T(8,128)(2,1)}) %all-gather.23.cloned.1.call-update) | async-done | bytes 2359312 | tf_op jit(solution)/shard_map/all_gather | solution.py:114
  925.7 3.2 convolution_multiply_fusion
  (70 shorter events, 15.2 us)
Async XLA Ops:
  7.2 94.6 %reduce-scatter.7.cloned.1.call-start = ((), (), s32[]{:S(2)}) async-start(), calls=%async_computation.8 | async-start | bytes 2506752 | tf_op jit(solution)/shard_map/reduce_scatter | solution.py:43
  21.0 80.8 %copy-start.8 = (f32[192,384]{1,0:T(8,128)S(1)}, f32[192,384]{1,0:T(8,128)}, u32[]{:S(2)}) copy-start(f32[192,384]{1,0:T(8,128)} %param.11) | copy-start | bytes 884740
  24.1 79.5 %copy-start.9 = (f32[192,384]{1,0:T(8,128)S(1)}, f32[192,384]{1,0:T(8,128)}, u32[]{:S(2)}) copy-start(f32[192,384]{1,0:T(8,128)} %param.13) | copy-start | bytes 884740
  24.1 104.8 %all-gather.13.cloned.1.call-start = ((), (), s32[]{:S(2)}) async-start(), calls=%async_computation.11 | async-start | bytes 2654208 | tf_op jit(solution)/shard_map/all_gather | solution.py:73
  103.5 82.6 %all-gather.15.cloned.1.call-start = ((), (), s32[]{:S(2)}) async-start(), calls=%async_computation.12 | async-start | bytes 5013504 | tf_op jit(solution)/shard_map/all_gather | solution.py:76
  104.4 176.5 %all-gather.17.cloned.1.call-start = ((), (), s32[]{:S(2)}) async-start(), calls=%async_computation.13 | async-start | bytes 1327104 | tf_op jit(solution)/shard_map/all_gather | solution.py:102
  259.8 102.5 %copy-start.7 = (bf16[48,384]{1,0:T(8,128)(2,1)S(1)}, bf16[48,384]{1,0:T(8,128)(2,1)}, u32[]{:S(2)}) copy-start(bf16[48,384]{1,0:T(8,128)(2,1)} %param.7) | copy-start | bytes 110596
  259.8 100.7 %reduce-scatter.9.cloned.1.call-start = ((), (), s32[]{:S(2)}) async-start(), calls=%async_computation.14 | async-start | bytes 2506752 | tf_op jit(solution)/shard_map/reduce_scatter | solution.py:103
  284.6 124.2 %copy-start.4 = (bf16[192,3072]{1,0:T(8,128)(2,1)S(1)}, bf16[192,3072]{1,0:T(8,128)(2,1)}, u32[]{:S(2)}) copy-start(bf16[192,3072]{1,0:T(8,128)(2,1)} %all-gather.17.cloned.1.call-done) | copy-start | bytes 3538948
  284.6 124.1 %all-gather.19.cloned.1.call-start = ((), (), s32[]{:S(2)}) async-start(), calls=%async_computation.15 | async-start | bytes 2506752 | tf_op jit(solution)/shard_map/all_gather | solution.py:114
  362.3 103.5 %all-reduce.4.cloned.1.call-start = ((), (), s32[]{:S(2)}) async-start(), calls=%async_computation.7 | async-start | bytes 147456 | tf_op jit(solution)/shard_map/psum | solution.py:40
  386.9 127.0 %all-gather.9.cloned.1.call-start = ((), (), s32[]{:S(2)}) async-start(), calls=%async_computation.4 | async-start | bytes 2506752 | tf_op jit(solution)/shard_map/all_gather | solution.py:50
  387.6 78.2 %copy-start.10 = (f32[48,768]{1,0:T(8,128)S(1)}, f32[48,768]{1,0:T(8,128)}, u32[]{:S(2)}) copy-start(f32[48,768]{1,0:T(8,128)} %param.10) | copy-start | bytes 442372
  387.6 173.0 %all-gather.21.cloned.1.call-start = ((), (), s32[]{:S(2)}) async-start(), calls=%async_computation.16 | async-start | bytes 1327104 | tf_op jit(solution)/shard_map/all_gather | solution.py:102
  411.9 175.4 %all-gather.11.cloned.1.call-start = ((), (), s32[]{:S(2)}) async-start(), calls=%async_computation.5 | async-start | bytes 2506752 | tf_op jit(solution)/shard_map/all_gather | solution.py:60
  412.5 264.9 %all-reduce.6.cloned.1.call-start = ((), (), s32[]{:S(2)}) async-start(), calls=%async_computation.9 | async-start | bytes 2359296 | tf_op jit(solution)/shard_map/psum | solution.py:92
  466.7 93.9 %copy-start.6 = (f32[48,768]{1,0:T(8,128)}, f32[48,768]{1,0:T(8,128)S(1)}, u32[]{:S(2)}) copy-start(f32[48,768]{1,0:T(8,128)S(1)} %multiply_add_fusion.1) | copy-start | bytes 442372
  466.7 93.9 %copy-start.5 = (bf16[192,384]{1,0:T(8,128)(2,1)S(1)}, bf16[192,384]{1,0:T(8,128)(2,1)}, u32[]{:S(2)}) copy-start(bf16[192,384]{1,0:T(8,128)(2,1)} %convolution_convert_fusion.5) | copy-start | bytes 442372
  560.6 4.1 copy-start
  560.6 195.2 %reduce-scatter.11.cloned.1.call-start = ((), (), s32[]{:S(2)}) async-start(), calls=%async_computation.17 | async-start | bytes 2506752 | tf_op jit(solution)/shard_map/reduce_scatter | solution.py:103
  564.6 22.6 %copy-start.11 = (f32[48,384]{1,0:T(8,128)S(1)}, f32[48,384]{1,0:T(8,128)}, u32[]{:S(2)}) copy-start(f32[48,384]{1,0:T(8,128)} %param.8) | copy-start | bytes 221188
  564.6 22.6 %copy-start.12 = (f32[48,384]{1,0:T(8,128)S(1)}, f32[48,384]{1,0:T(8,128)}, u32[]{:S(2)}) copy-start(f32[48,384]{1,0:T(8,128)} %param.9) | copy-start | bytes 221188
  564.6 224.3 %reduce-scatter.5.cloned.1.call-start = ((), (), s32[]{:S(2)}) async-start(), calls=%async_computation.6 | async-start | bytes 663552 | tf_op jit(solution)/shard_map/reduce_scatter | solution.py:70
  564.9 1.0 copy-start.2
  587.3 27.3 %copy-start.1 = (bf16[3072,384]{1,0:T(8,128)(2,1)S(1)}, bf16[3072,384]{1,0:T(8,128)(2,1)}, u32[]{:S(2)}) copy-start(bf16[3072,384]{1,0:T(8,128)(2,1)} %all-gather.11.cloned.1.call-done) | copy-start | bytes 7077892
  617.3 260.7 %all-reduce.8.cloned.1.call-start = ((), (), s32[]{:S(2)}) async-start(), calls=%async_computation.10 | async-start | bytes 2359296 | tf_op jit(solution)/shard_map/psum | solution.py:92
  679.4 246.3 %copy-start.3 = (bf16[192,3072]{1,0:T(8,128)(2,1)S(1)}, bf16[192,3072]{1,0:T(8,128)(2,1)}, u32[]{:S(2)}) copy-start(bf16[192,3072]{1,0:T(8,128)(2,1)} %all-gather.21.cloned.1.call-done) | copy-start | bytes 3538948
  682.5 243.1 %all-gather.23.cloned.1.call-start = ((), (), s32[]{:S(2)}) async-start(), calls=%async_computation.18 | async-start | bytes 2506752 | tf_op jit(solution)/shard_map/all_gather | solution.py:114
Sparse Core Ops, SparseCore 0:
  24.2 77.5 reduce-scatter.6
  104.0 24.8 all-gather.12
  131.6 54.4 all-gather.14
  260.0 20.8 all-gather.16
  284.7 75.7 reduce-scatter.8
  363.1 45.5 all-gather.18
  411.6 54.1 all-reduce.3
  468.0 45.9 all-gather.8
  516.2 22.8 all-gather.20
  541.6 45.6 all-gather.10
  590.6 86.8 all-reduce.5
  680.6 75.1 reduce-scatter.10
  758.2 30.7 reduce-scatter.4
  792.1 85.8 all-reduce.7
  880.6 45.0 all-gather.22
where the time goes:
time: 936 us; the launch traced here: 935 us
  waiting for transfers between devices  684 us (73%)
  blocking collectives  179 us (19%)
  matrix products  46.3 us (5%)
  between operations  15.6 us (2%)
    reduce_scatter x2, waiting for transfers between devices, local(): lax.psum_scatter(jnp.dot(iterate_rows.T, rounded_iterate, preferred_eleme...  149 us
    psum x2, waiting for transfers between devices, local(): lax.psum(partial_gram.astype(jnp.bfloat16), 'shard').astype(jnp.float32)  148 us
    reduce_scatter x1, waiting for transfers between devices, local(): lax.psum_scatter(jnp.dot(grad_rows.T, gradient, preferred_element_type=jn...  77.6 us
    all_gather x2, waiting for transfers between devices, local(): lax.all_gather(mixing, 'shard', axis=0, tiled=True)  66 us
    psum x1, blocking collectives, local(): total_right = lax.psum(local_right, ('shard', 'tensor'))  64.5 us
    all_gather x1, waiting for transfers between devices, local(): lax.all_gather(right_q, 'shard', axis=0, tiled=True)  57.2 us
    psum x1, waiting for transfers between devices, local(): lax.psum(left_terms.astype(jnp.bfloat16), 'tensor').astype(jnp.float32)  53.3 us
    all_gather x1, waiting for transfers between devices, local(): basis_all = lax.all_gather(basis_left, 'shard', axis=0, tiled=True)  47.2 us
  transfers between devices with their start and end apart: 15, of which 14 were waited for; matrix products, arithmetic and copies ran while one was open for 4% of the time, Pallas kernels for 0%

commit v1 on v0

--- a/solution.py
+++ b/solution.py
@@ -13,6 +13,11 @@
 correction = 1.0 - 0.95**10
 adam_eps = 1e-08
 highest = lax.Precision.HIGHEST
+
+
+def add_all(x, axis):
+    shards = lax.all_gather(x, axis)
+    return jnp.sum(shards, axis=0)
 
 
 def blend_stat(previous, product, divisor):
@@ -37,7 +42,7 @@
     row_start = shard_pos * rows_left
     grad_cols = lax.all_gather(gradient, "shard", axis=0, tiled=True)
     left_terms = jnp.dot(gradient, grad_cols.T, preferred_element_type=jnp.float32)
-    gram_rows = lax.psum(left_terms.astype(jnp.bfloat16), "tensor").astype(jnp.float32)
+    gram_rows = add_all(left_terms.astype(jnp.bfloat16), "tensor").astype(jnp.float32)
     new_stat_left = blend_stat(stat_left, gram_rows, FF)
     grad_rows = lax.all_gather(gradient, "tensor", axis=1, tiled=True)
     gram_block = lax.psum_scatter(

time: 936 us -> 878 us (0.938)
  waiting for transfers between devices: 684 us -> 613 us
  blocking collectives: 179 us -> 193 us
    psum x1 -> x0, waiting for transfers between devices: 53.3 us -> none  [local(): lax.psum(left_terms.astype(jnp.bfloat16), 'tensor').astype(jnp.float32)]
    all_gather x1, waiting for transfers between devices: 47.2 us -> 5.34 us  [local(): basis_all = lax.all_gather(basis_left, 'shard', axis=0, tiled=True)]
    all_gather x2, waiting for transfers between devices: 66 us -> 89.9 us  [local(): lax.all_gather(mixing, 'shard', axis=0, tiled=True)]
    all_gather x0 -> x1, blocking collectives: none -> 13.5 us  [add_all(): shards = lax.all_gather(x, axis)]
  transfers between devices with their start and end apart: 15 -> 14, of which waited for: 14 -> 13; matrix products, arithmetic and copies ran while one was open for 4% -> 4% of each run, Pallas kernels for 0% -> 0%
where the time goes in v1:
time: 878 us; the launch traced here: 877 us
  waiting for transfers between devices  613 us (70%)
  blocking collectives  193 us (22%)
  matrix products  45.7 us (5%)
  between operations  15.6 us (2%)
    reduce_scatter x2, waiting for transfers between devices, local(): lax.psum_scatter(jnp.dot(iterate_rows.T, rounded_iterate, preferred_eleme...  149 us
    psum x2, waiting for transfers between devices, local(): lax.psum(partial_gram.astype(jnp.bfloat16), 'shard').astype(jnp.float32)  148 us
    all_gather x2, waiting for transfers between devices, local(): lax.all_gather(mixing, 'shard', axis=0, tiled=True)  89.9 us
    reduce_scatter x1, waiting for transfers between devices, local(): lax.psum_scatter(jnp.dot(grad_rows.T, gradient, preferred_element_type=jn...  77.5 us
    psum x1, blocking collectives, local(): total_right = lax.psum(local_right, ('shard', 'tensor'))  64.5 us
    all_gather x1, waiting for transfers between devices, local(): lax.all_gather(right_q, 'shard', axis=0, tiled=True)  57.2 us
    psum x1, blocking collectives, local(): total_left = lax.psum(local_left, 'shard')  39.1 us
    reduce_scatter x1, waiting for transfers between devices, local(): lax.psum_scatter(back_terms, 'tensor', scatter_dimension=1, tiled=True)  31.3 us
  transfers between devices with their start and end apart: 14, of which 13 were waited for; matrix products, arithmetic and copies ran while one was open for 4% of the time, Pallas kernels for 0%

profile of v1, /device:TPU:0, one launch (start us, length us, event | category | flops | bytes accessed | tf_op | source)
XLA Modules:
  0.0 877.2 jit_solution(11943040214229783819)
XLA Ops:
  7.2 13.8 %all_gather.49 = bf16[48,3072]{1,0:T(8,128)(2,1)S(1)} all-gather(bf16[48,384]{1,0:T(8,128)(2,1)} %param.7), channel_id=1, replica_groups=mesh['shard'=16,'tensor'=8] {'tensor'}, dimensions={1}, use_global_device_ids=true | all-gather | bytes 331776 | tf_op jit(solution)/shard_map/all_gather | solution.py:47
  21.0 3.1 convolution_convert_fusion.2
  24.2 77.5 %reduce-scatter.7.cloned.1.call-done = bf16[192,384]{1,0:T(8,128)(2,1)} async-done(((bf16[3072,384]{1,0:T(8,128)(2,1)}), bf16[192,384]{1,0:T(8,128)(2,1)}) %reduce-scatter.7.cloned.1.call-update) | async-done | bytes 147472 | tf_op jit(solution)/shard_map/reduce_scatter | solution.py:48
  104.3 24.5 %all-gather.14.cloned.1.call-done = f32[192,3072]{1,0:T(8,128)} async-done(((f32[192,384]{1,0:T(8,128)}), f32[192,3072]{1,0:T(8,128)}) %all-gather.14.cloned.1.call-update) | async-done | bytes 2359312 | tf_op jit(solution)/shard_map/all_gather | solution.py:78
  128.8 57.2 %all-gather.16.cloned.1.call-done = f32[3072,384]{1,0:T(8,128)} async-done(((f32[192,384]{1,0:T(8,128)}), f32[3072,384]{1,0:T(8,128)}) %all-gather.16.cloned.1.call-update) | async-done | bytes 4718608 | tf_op jit(solution)/shard_map/all_gather | solution.py:81
  185.9 7.8 multiply_reduce_fusion
  193.7 64.5 %psum.31 = f32[]{:T(128)} all-reduce(f32[]{:T(128)} %get-tuple-element.14), channel_id=1, replica_groups=mesh['shard'=16,'tensor'=8] {'shard','tensor'}, use_global_device_ids=true, to_apply=%region_8.0 | all-reduce | flops 1 | bytes 8 | tf_op jit(solution)/shard_map/psum | solution.py:91
  259.8 21.0 %all-gather.18.cloned.1.call-done = bf16[192,3072]{1,0:T(8,128)(2,1)} async-done(((bf16[192,384]{1,0:T(8,128)(2,1)}), bf16[192,3072]{1,0:T(8,128)(2,1)}) %all-gather.18.cloned.1.call-update) | async-done | bytes 1179664 | tf_op jit(solution)/shard_map/all_gather | solution.py:107
  280.7 3.8 convolution_convert_fusion.1
  284.6 75.8 %reduce-scatter.9.cloned.1.call-done = bf16[192,384]{1,0:T(8,128)(2,1)} async-done(((bf16[3072,384]{1,0:T(8,128)(2,1)}), bf16[192,384]{1,0:T(8,128)(2,1)}) %reduce-scatter.9.cloned.1.call-update) | async-done | bytes 147472 | tf_op jit(solution)/shard_map/reduce_scatter | solution.py:108
  362.9 44.9 %all-gather.20.cloned.1.call-done = bf16[3072,384]{1,0:T(8,128)(2,1)} async-done(((bf16[192,384]{1,0:T(8,128)(2,1)}), bf16[3072,384]{1,0:T(8,128)(2,1)}) %all-gather.20.cloned.1.call-update) | async-done | bytes 2359312 | tf_op jit(solution)/shard_map/all_gather | solution.py:119
  407.8 3.1 convolution_convert_fusion.5
  411.8 24.2 %all_gather.43 = bf16[768,384]{1,0:T(8,128)(2,1)S(1)} all-gather(bf16[48,384]{1,0:T(8,128)(2,1)S(1)} %copy-done.7), channel_id=1, replica_groups=mesh['shard'=16,'tensor'=8] {'shard'}, dimensions={0}, use_global_device_ids=true | all-gather | bytes 626688 | tf_op jit(solution)/shard_map/all_gather | solution.py:43
  436.3 13.5 %all-gather = bf16[384,768]{1,0:T(8,128)(2,1)S(1)} all-gather(bf16[48,768]{1,0:T(8,128)(2,1)S(1)} %convolution_convert_fusion.6), channel_id=2, replica_groups=mesh['shard'=16,'tensor'=8] {'tensor'}, dimensions={0}, use_global_device_ids=true | all-gather | bytes 663552 | tf_op jit(solution)/shard_map/all_gather | solution.py:19
  450.0 5.3 all-gather.10.cloned.1.call-done
  455.3 3.8 multiply_reduce_fusion.1
  459.2 39.1 %psum.28 = f32[]{:T(128)} all-reduce(f32[]{:T(128)} %get-tuple-element.12), channel_id=1, replica_groups=mesh['shard'=16,'tensor'=8] {'shard'}, use_global_device_ids=true, to_apply=%region_4.0 | all-reduce | flops 1 | bytes 8 | tf_op jit(solution)/shard_map/psum | solution.py:90
  498.9 3.1 convolution_convert_fusion.4
  502.2 3.9 convolution_convert_fusion
  507.4 13.3 %all_gather.44 = bf16[48,3072]{1,0:T(8,128)(2,1)S(1)} all-gather(bf16[48,384]{1,0:T(8,128)(2,1)S(1)} %convolution_convert_fusion.8), channel_id=1, replica_groups=mesh['shard'=16,'tensor'=8] {'tensor'}, dimensions={1}, use_global_device_ids=true | all-gather | bytes 331776 | tf_op jit(solution)/shard_map/all_gather | solution.py:66
  520.7 8.1 all-gather.12.cloned.1.call-done
  528.8 3.0 divide_convert_fusion
  531.8 24.5 %all_gather.46 = bf16[768,384]{1,0:T(8,128)(2,1)S(1)} all-gather(bf16[48,384]{1,0:T(8,128)(2,1)S(1)} %get-tuple-element.7), channel_id=1, replica_groups=mesh['shard'=16,'tensor'=8] {'shard'}, dimensions={0}, use_global_device_ids=true | all-gather | bytes 626688 | tf_op jit(solution)/shard_map/all_gather | solution.py:71
  556.3 2.7 fusion.6
  559.1 59.9 %all-reduce.3.cloned.1.call-done = bf16[768,768]{1,0:T(8,128)(2,1)} async-done(((bf16[768,768]{1,0:T(8,128)(2,1)}), bf16[768,768]{1,0:T(8,128)(2,1)}) %all-reduce.3.cloned.1.call-update) | async-done | bytes 1179664 | tf_op jit(solution)/shard_map/psum | solution.py:97
  621.0 3.1 convolution_convert_fusion.3
  624.1 73.4 %reduce-scatter.11.cloned.1.call-done = bf16[192,384]{1,0:T(8,128)(2,1)} async-done(((bf16[3072,384]{1,0:T(8,128)(2,1)}), bf16[192,384]{1,0:T(8,128)(2,1)}) %reduce-scatter.11.cloned.1.call-update) | async-done | bytes 147472 | tf_op jit(solution)/shard_map/reduce_scatter | solution.py:108
  699.2 31.3 %reduce-scatter.5.cloned.1.call-done = f32[48,384]{1,0:T(8,128)} async-done(((f32[48,3072]{1,0:T(8,128)}), f32[48,384]{1,0:T(8,128)}) %reduce-scatter.5.cloned.1.call-update) | async-done | bytes 73744 | tf_op jit(solution)/shard_map/reduce_scatter | solution.py:75
  732.0 87.8 %all-reduce.5.cloned.1.call-done = bf16[768,768]{1,0:T(8,128)(2,1)} async-done(((bf16[768,768]{1,0:T(8,128)(2,1)}), bf16[768,768]{1,0:T(8,128)(2,1)}) %all-reduce.5.cloned.1.call-update) | async-done | bytes 1179664 | tf_op jit(solution)/shard_map/psum | solution.py:97
  819.9 2.6 fusion.4
  822.5 45.0 %all-gather.24.cloned.1.call-done = bf16[3072,384]{1,0:T(8,128)(2,1)} async-done(((bf16[192,384]{1,0:T(8,128)(2,1)}), bf16[3072,384]{1,0:T(8,128)(2,1)}) %all-gather.24.cloned.1.call-update) | async-done | bytes 2359312 | tf_op jit(solution)/shard_map/all_gather | solution.py:119
  867.5 3.2 convolution_multiply_fusion
  (69 shorter events, 13.9 us)
Async XLA Ops:
  7.2 94.5 %reduce-scatter.7.cloned.1.call-start = ((), (), s32[]{:S(2)}) async-start(), calls=%async_computation.7 | async-start | bytes 2506752 | tf_op jit(solution)/shard_map/reduce_scatter | solution.py:48
  21.0 80.7 %copy-start.8 = (f32[192,384]{1,0:T(8,128)S(1)}, f32[192,384]{1,0:T(8,128)}, u32[]{:S(2)}) copy-start(f32[192,384]{1,0:T(8,128)} %param.11) | copy-start | bytes 884740
  24.1 79.3 %copy-start.9 = (f32[192,384]{1,0:T(8,128)S(1)}, f32[192,384]{1,0:T(8,128)}, u32[]{:S(2)}) copy-start(f32[192,384]{1,0:T(8,128)} %param.13) | copy-start | bytes 884740
  24.1 104.7 %all-gather.14.cloned.1.call-start = ((), (), s32[]{:S(2)}) async-start(), calls=%async_computation.10 | async-start | bytes 2654208 | tf_op jit(solution)/shard_map/all_gather | solution.py:78
  103.3 82.6 %all-gather.16.cloned.1.call-start = ((), (), s32[]{:S(2)}) async-start(), calls=%async_computation.11 | async-start | bytes 5013504 | tf_op jit(solution)/shard_map/all_gather | solution.py:81
  104.2 176.5 %all-gather.18.cloned.1.call-start = ((), (), s32[]{:S(2)}) async-start(), calls=%async_computation.12 | async-start | bytes 1327104 | tf_op jit(solution)/shard_map/all_gather | solution.py:107
  259.7 100.7 %reduce-scatter.9.cloned.1.call-start = ((), (), s32[]{:S(2)}) async-start(), calls=%async_computation.13 | async-start | bytes 2506752 | tf_op jit(solution)/shard_map/reduce_scatter | solution.py:108
  284.5 123.4 %copy-start.4 = (bf16[192,3072]{1,0:T(8,128)(2,1)S(1)}, bf16[192,3072]{1,0:T(8,128)(2,1)}, u32[]{:S(2)}) copy-start(bf16[192,3072]{1,0:T(8,128)(2,1)} %all-gather.18.cloned.1.call-done) | copy-start | bytes 3538948
  284.5 123.3 %all-gather.20.cloned.1.call-start = ((), (), s32[]{:S(2)}) async-start(), calls=%async_computation.14 | async-start | bytes 2506752 | tf_op jit(solution)/shard_map/all_gather | solution.py:119
  362.1 93.2 %all-gather.10.cloned.1.call-start = ((), (), s32[]{:S(2)}) async-start(), calls=%async_computation.4 | async-start | bytes 2506752 | tf_op jit(solution)/shard_map/all_gather | solution.py:55
  362.9 48.9 %copy-start.7 = (bf16[48,384]{1,0:T(8,128)(2,1)S(1)}, bf16[48,384]{1,0:T(8,128)(2,1)}, u32[]{:S(2)}) copy-start(bf16[48,384]{1,0:T(8,128)(2,1)} %param.7) | copy-start | bytes 110596
  362.9 139.3 %all-gather.22.cloned.1.call-start = ((), (), s32[]{:S(2)}) async-start(), calls=%async_computation.15 | async-start | bytes 1327104 | tf_op jit(solution)/shard_map/all_gather | solution.py:107
  410.9 39.0 %copy-start.10 = (f32[48,768]{1,0:T(8,128)S(1)}, f32[48,768]{1,0:T(8,128)}, u32[]{:S(2)}) copy-start(f32[48,768]{1,0:T(8,128)} %param.10) | copy-start | bytes 442372
  411.0 117.8 %all-gather.12.cloned.1.call-start = ((), (), s32[]{:S(2)}) async-start(), calls=%async_computation.5 | async-start | bytes 2506752 | tf_op jit(solution)/shard_map/all_gather | solution.py:65
  411.7 207.3 %all-reduce.3.cloned.1.call-start = ((), (), s32[]{:S(2)}) async-start(), calls=%async_computation.8 | async-start | bytes 2359296 | tf_op jit(solution)/shard_map/psum | solution.py:97
  450.0 52.1 %copy-start.6 = (f32[48,768]{1,0:T(8,128)}, f32[48,768]{1,0:T(8,128)S(1)}, u32[]{:S(2)}) copy-start(f32[48,768]{1,0:T(8,128)S(1)} %multiply_add_fusion.1) | copy-start | bytes 442372
  450.0 52.2 %copy-start.5 = (bf16[192,384]{1,0:T(8,128)(2,1)S(1)}, bf16[192,384]{1,0:T(8,128)(2,1)}, u32[]{:S(2)}) copy-start(bf16[192,384]{1,0:T(8,128)(2,1)} %convolution_convert_fusion.5) | copy-start | bytes 442372
  502.1 4.1 copy-start
  502.1 195.4 %reduce-scatter.11.cloned.1.call-start = ((), (), s32[]{:S(2)}) async-start(), calls=%async_computation.16 | async-start | bytes 2506752 | tf_op jit(solution)/shard_map/reduce_scatter | solution.py:108
  506.1 22.7 %copy-start.11 = (f32[48,384]{1,0:T(8,128)S(1)}, f32[48,384]{1,0:T(8,128)}, u32[]{:S(2)}) copy-start(f32[48,384]{1,0:T(8,128)} %param.8) | copy-start | bytes 221188
  506.1 22.7 %copy-start.12 = (f32[48,384]{1,0:T(8,128)S(1)}, f32[48,384]{1,0:T(8,128)}, u32[]{:S(2)}) copy-start(f32[48,384]{1,0:T(8,128)} %param.9) | copy-start | bytes 221188
  506.1 224.4 %reduce-scatter.5.cloned.1.call-start = ((), (), s32[]{:S(2)}) async-start(), calls=%async_computation.6 | async-start | bytes 663552 | tf_op jit(solution)/shard_map/reduce_scatter | solution.py:75
  506.4 1.0 copy-start.2
  528.8 27.5 %copy-start.1 = (bf16[3072,384]{1,0:T(8,128)(2,1)S(1)}, bf16[3072,384]{1,0:T(8,128)(2,1)}, u32[]{:S(2)}) copy-start(bf16[3072,384]{1,0:T(8,128)(2,1)} %all-gather.12.cloned.1.call-done) | copy-start | bytes 7077892
  559.0 260.8 %all-reduce.5.cloned.1.call-start = ((), (), s32[]{:S(2)}) async-start(), calls=%async_computation.9 | async-start | bytes 2359296 | tf_op jit(solution)/shard_map/psum | solution.py:97
  621.0 246.5 %copy-start.3 = (bf16[192,3072]{1,0:T(8,128)(2,1)S(1)}, bf16[192,3072]{1,0:T(8,128)(2,1)}, u32[]{:S(2)}) copy-start(bf16[192,3072]{1,0:T(8,128)(2,1)} %all-gather.22.cloned.1.call-done) | copy-start | bytes 3538948
  624.1 243.4 %all-gather.24.cloned.1.call-start = ((), (), s32[]{:S(2)}) async-start(), calls=%async_computation.17 | async-start | bytes 2506752 | tf_op jit(solution)/shard_map/all_gather | solution.py:119
Sparse Core Ops, SparseCore 0:
  24.2 77.3 reduce-scatter.6
  103.9 24.8 all-gather.13
  131.5 54.4 all-gather.15
  259.8 20.8 all-gather.17
  284.6 75.7 reduce-scatter.8
  363.0 44.8 all-gather.19
  410.0 45.2 all-gather.9
  457.6 22.8 all-gather.21
  483.2 45.6 all-gather.11
  531.9 86.9 all-reduce.2
  622.3 75.1 reduce-scatter.10
  699.7 30.7 reduce-scatter.4
  733.8 85.9 all-reduce.4
  822.4 45.0 all-gather.23
